TPU v7x, 32 devices: a whole 2x2x4 slice. The times are simulated.
32 devices in a mesh: grp: 2 (over y), smp: 4 (over z), mrk: 4 (over x, core).
Axes of the slice: x: 2, y: 2, z: 4, core: 2. Of those that a mesh axis runs over, the one named last changes fastest.
Arguments:
- genotypes: bfloat16 [4096, 16384], P('smp', ('grp', 'mrk')), parts along dimension 1, may hold values from 0 to 2, as said below
- effect_class: int32 [16384], P(('grp', 'mrk')), parts along dimension 0, may hold values from 0 to 511
- effect_table: bfloat16 [1024, 256], P('grp'), parts along dimension 0, may hold values from -0.0625 to 0.0625
Outputs:
- assoc: float32 [256, 16384], P('smp', ('grp', 'mrk')), parts along dimension 1
There are 2 independent parts, one for each index of `grp`. A program takes and returns all parts, laid end to end along the dimension named above; each array names one. Nothing has to cross between parts.
Inputs may be any that keep to these rules, and one draw needn't show every extreme that they name: `genotypes`: dosages are whole numbers.
All inputs are finite; a program needn't handle non-finite values.
Results may differ from a plain program's by a relative error of at most 0.0032.
Values may be sent and summed in bfloat16 or wider, within the bound.
No kernel may reach another device: no remote copies, remote signals or barrier semaphores. Data moves between devices by JAX's collectives and lax.ppermute only.
A program may use at most 64 MiB of HBM per device.

v0:
```python
import math
import jax
import jax.numpy as jnp
from jax import lax
from jax.sharding import PartitionSpec as P

BLK_DEV = 1024
NBLK = 2
EPSILON = 1e-05


def marker_moments(genotypes, samples):
    totals = jnp.sum(genotypes, axis=0, dtype=jnp.float32)
    center = lax.psum(totals, "smp") / samples
    local_squares = jnp.sum(jnp.square(genotypes.astype(jnp.float32) - center[None, :]), axis=0)
    spread = lax.psum(local_squares, "smp") / samples
    return lax.rsqrt(spread + EPSILON)


def standardize(phenotype, samples):
    totals = jnp.sum(phenotype, axis=0)
    center = lax.psum(totals, "smp") / samples
    local_squares = jnp.sum(jnp.square(phenotype - center[None, :]), axis=0)
    spread = lax.psum(local_squares, "smp") / samples
    return ((phenotype - center[None, :]) * lax.rsqrt(spread + EPSILON)[None, :]).astype(
        jnp.bfloat16
    )


def shards(genotypes, effect_class, effect_table):
    samples = genotypes.shape[0] * lax.axis_size("smp")
    markers_here = genotypes.shape[1]
    inverse_spread = marker_moments(genotypes, samples)
    classes_iota = lax.broadcasted_iota(jnp.int32, (markers_here, effect_table.shape[0]), 1)
    onehot = (effect_class[:, None] == classes_iota).astype(jnp.bfloat16)
    effects = jnp.dot(onehot, effect_table, preferred_element_type=jnp.float32)
    scaled = (effects * inverse_spread[:, None]).astype(jnp.bfloat16)
    partial_sum = jnp.dot(genotypes, scaled, preferred_element_type=jnp.float32)
    phenotype = lax.psum(partial_sum, "mrk")
    standard = standardize(phenotype, samples)
    root_count = math.sqrt(samples)
    pieces = []
    for block_index in range(NBLK):
        columns = genotypes[:, block_index * BLK_DEV : (block_index + 1) * BLK_DEV]
        pieces.append(
            lax.psum_scatter(
                lax.dot_general(
                    standard, columns, (((0,), (0,)), ((), ())), preferred_element_type=jnp.float32
                ),
                "smp",
                scatter_dimension=0,
                tiled=True,
            )
        )
    summed = jnp.concatenate(pieces, axis=1)
    return summed * inverse_spread[None, :] / root_count


def solution(mesh):
    return jax.shard_map(
        shards,
        mesh=mesh,
        in_specs=(P("smp", ("grp", "mrk")), P(("grp", "mrk")), P("grp", None)),
        out_specs=P("smp", ("grp", "mrk")),
        check_vma=False,
    )
```

profile of v0, /device:TPU:0, one launch (start us, length us, event | category | flops | bytes accessed | tf_op | source)
XLA Modules:
  0.0 166.8 jit_solution(4051340667754941652)
XLA Ops:
  6.5 0.0 copy-start
  6.5 0.0 all-reduce.2.cloned.1.call-start
  6.5 2.9 %convert_reduce_fusion = f32[2048]{0:T(1024)S(1)} fusion(bf16[1024,2048]{1,0:T(8,128)(2,1)} %param.3), kind=kLoop, calls=%fused_computation.1 | loop fusion | flops 4192256 | bytes 4202496 | tf_op jit(solution)/shard_map/reduce_sum | solution.py:13
  9.4 13.7 %psum.35 = f32[2048]{0:T(1024)S(1)} all-reduce(f32[2048]{0:T(1024)S(1)} %convert_reduce_fusion), channel_id=1, replica_groups=mesh['grp'=2,'smp'=4,'mrk'=4] {'smp'}, use_global_device_ids=true, to_apply=%region_1.0 | all-reduce | flops 2048 | bytes 16384 | tf_op jit(solution)/shard_map/psum | solution.py:14
  23.2 3.3 %fusion.1 = f32[2048]{0:T(1024)S(1)} fusion(bf16[1024,2048]{1,0:T(8,128)(2,1)} %param.3, f32[2048]{0:T(1024)S(1)} %broadcast_multiply_fusion), kind=kLoop, calls=%fused_computation.3 | loop fusion | flops 8386560 | bytes 4210688 | tf_op jit(solution)/shard_map/reduce_sum | solution.py:15
  26.5 8.5 %psum.36 = f32[2048]{0:T(1024)S(1)} all-reduce(f32[2048]{0:T(1024)S(1)} %fusion.1), channel_id=1, replica_groups=mesh['grp'=2,'smp'=4,'mrk'=4] {'smp'}, use_global_device_ids=true, to_apply=%region_3.0 | all-reduce | flops 2048 | bytes 16384 | tf_op jit(solution)/shard_map/psum | solution.py:16
  35.0 0.0 copy-done
  35.0 0.0 copy-done.2
  35.1 5.8 %convolution_bitcast_fusion = f32[1024,256]{0,1:T(8,128)} fusion(bf16[1024,2048]{1,0:T(8,128)(2,1)} %param.3, bf16[512,256]{1,0:T(8,128)(2,1)S(1)} %copy-done, s32[2048]{0:T(1024)S(1)} %copy-done.2, f32[2048]{0:T(1024)S(1)} %add_rsqrt_fusion), kind=kOutput, calls=%fused_computation.13 | convolution fusion | flops 1612709888 | bytes 5521408 | tf_op jit(solution)/shard_map/dot_general | solution.py:38
  40.8 0.0 all-reduce.2.cloned.1.call-update
  40.8 0.0 reduce-scatter.3.cloned.1.call-start
  40.9 36.1 %all-reduce.2.cloned.1.call-done = f32[1024,256]{0,1:T(8,128)} async-done(((f32[1024,256]{0,1:T(8,128)}), f32[1024,256]{0,1:T(8,128)}) %all-reduce.2.cloned.1.call-update) | async-done | bytes 1048592 | tf_op jit(solution)/shard_map/psum | solution.py:39
  77.0 1.4 reduce_sum.38
  78.4 11.7 %psum.38 = f32[256]{0:T(256)S(1)} all-reduce(f32[256]{0:T(256)S(1)} %reduce_sum.38), channel_id=1, replica_groups=mesh['grp'=2,'smp'=4,'mrk'=4] {'smp'}, use_global_device_ids=true, to_apply=%region_6.0 | all-reduce | flops 256 | bytes 2048 | tf_op jit(solution)/shard_map/psum | solution.py:22
  90.1 1.5 multiply_reduce_fusion
  91.6 8.4 %psum.39 = f32[256]{0:T(256)S(1)} all-reduce(f32[256]{0:T(256)S(1)} %multiply_reduce_fusion), channel_id=1, replica_groups=mesh['grp'=2,'smp'=4,'mrk'=4] {'smp'}, use_global_device_ids=true, to_apply=%region_8.0 | all-reduce | flops 256 | bytes 2048 | tf_op jit(solution)/shard_map/psum | solution.py:24
  100.0 3.7 %fusion.7 = f32[256,1024]{1,0:T(8,128)} fusion(bf16[1024,2048]{1,0:T(8,128)(2,1)} %param.3, f32[1024,256]{0,1:T(8,128)} %all-reduce.2.cloned.1.call-done, f32[256]{0:T(256)S(1)} %add_rsqrt_fusion.1, f32[256]{0:T(256)S(1)} %broadcast_multiply_fusion.1), kind=kOutput, calls=%fused_computation.10 | convolution fusion | flops 537657344 | bytes 4196352 | tf_op jit(solution)/shard_map/dot_general | solution.py:47
  103.6 0.0 reduce-scatter.3.cloned.1.call-update
  103.7 0.0 reduce-scatter.5.cloned.1.call-start
  103.7 3.4 %fusion.5 = f32[256,1024]{1,0:T(8,128)} fusion(bf16[1024,2048]{1,0:T(8,128)(2,1)} %param.3, f32[1024,256]{0,1:T(8,128)S(1)} %copy-done.1, f32[256]{0:T(256)S(1)} %add_rsqrt_fusion.1, f32[256]{0:T(256)S(1)} %broadcast_multiply_fusion.1), kind=kOutput, calls=%fused_computation.8 | convolution fusion | flops 537657344 | bytes 4196352 | tf_op jit(solution)/shard_map/dot_general | solution.py:47
  107.1 0.0 reduce-scatter.5.cloned.1.call-update
  107.1 23.1 %reduce-scatter.3.cloned.1.call-done = f32[64,1024]{1,0:T(8,128)} async-done(((f32[256,1024]{1,0:T(8,128)}), f32[64,1024]{1,0:T(8,128)}) %reduce-scatter.3.cloned.1.call-update) | async-done | bytes 262160 | tf_op jit(solution)/shard_map/reduce_scatter | solution.py:46
  130.3 28.1 %reduce-scatter.5.cloned.1.call-done = f32[64,1024]{1,0:T(8,128)} async-done(((f32[256,1024]{1,0:T(8,128)}), f32[64,1024]{1,0:T(8,128)}) %reduce-scatter.5.cloned.1.call-update) | async-done | bytes 262160 | tf_op jit(solution)/shard_map/reduce_scatter | solution.py:46
  158.4 1.9 %fusion.10 = f32[64,2048]{1,0:T(8,128)} fusion(f32[64,1024]{1,0:T(8,128)} %reduce-scatter.5.cloned.1.call-done, f32[64,1024]{1,0:T(8,128)} %reduce-scatter.3.cloned.1.call-done, f32[2048]{0:T(1024)S(1)} %add_rsqrt_fusion), kind=kLoop, calls=%fused_computation.17 | loop fusion | flops 393216 | bytes 1056768 | tf_op jit(solution)/shard_map/div | solution.py:56
  (7 shorter events, 0.0 us)
Async XLA Ops:
  6.5 28.5 %copy-start = (bf16[512,256]{1,0:T(8,128)(2,1)S(1)}, bf16[512,256]{1,0:T(8,128)(2,1)}, u32[]{:S(2)}) copy-start(bf16[512,256]{1,0:T(8,128)(2,1)} %param.5) | copy-start | bytes 786436
  6.5 28.5 %copy-start.2 = (s32[2048]{0:T(1024)S(1)}, s32[2048]{0:T(1024)}, u32[]{:S(2)}) copy-start(s32[2048]{0:T(1024)} %param.4) | copy-start | bytes 24580
  6.5 70.4 %all-reduce.2.cloned.1.call-start = ((), (), s32[]{:S(2)}) async-start(), calls=%async_computation.2 | async-start | bytes 2097152 | tf_op jit(solution)/shard_map/psum | solution.py:39
  40.8 89.4 %reduce-scatter.3.cloned.1.call-start = ((), (), s32[]{:S(2)}) async-start(), calls=%async_computation.3 | async-start | bytes 1310720 | tf_op jit(solution)/shard_map/reduce_scatter | solution.py:46
  77.0 26.8 %copy-start.1 = (f32[1024,256]{0,1:T(8,128)S(1)}, f32[1024,256]{0,1:T(8,128)}, u32[]{:S(2)}) copy-start(f32[1024,256]{0,1:T(8,128)} %all-reduce.2.cloned.1.call-done) | copy-start | bytes 3145732
  103.7 54.7 %reduce-scatter.5.cloned.1.call-start = ((), (), s32[]{:S(2)}) async-start(), calls=%async_computation.4 | async-start | bytes 1310720 | tf_op jit(solution)/shard_map/reduce_scatter | solution.py:46
Sparse Core Ops, SparseCore 0:
  41.0 35.9 all-reduce.1
  103.8 26.4 reduce-scatter.2
  132.6 25.7 reduce-scatter.4
where the time goes:
time: 167 us
  waiting for transfers between devices  87.4 us (52%)
  blocking collectives  42.3 us (25%)
  between operations  13.2 us (8%)
  matrix products  12.8 us (8%)
  other arithmetic  11 us (7%)
    reduce_scatter x2, waiting for transfers between devices, shards(): lax.psum_scatter(lax.dot_general(standard, columns, (((0,), (0,)), ((), (...  51.3 us
    psum x1, waiting for transfers between devices, shards(): phenotype = lax.psum(partial_sum, 'mrk')  36.1 us
    psum x1, blocking collectives, marker_moments(): center = lax.psum(totals, 'smp') / samples  13.7 us
    psum x1, blocking collectives, standardize(): center = lax.psum(totals, 'smp') / samples  11.7 us
    psum x1, blocking collectives, marker_moments(): spread = lax.psum(local_squares, 'smp') / samples  8.51 us
    psum x1, blocking collectives, standardize(): spread = lax.psum(local_squares, 'smp') / samples  8.37 us
    dot_general x2, matrix products, shards(): lax.dot_general(standard, columns, (((0,), (0,)), ((), ())), preferred_el...  7.07 us
    dot_general x1, matrix products, shards(): partial_sum = jnp.dot(genotypes, scaled, preferred_element_type=jnp.float32)  5.77 us
  transfers between devices with their start and end apart: 3, of which 3 were waited for; matrix products, arithmetic and copies ran while one was open for 2% of the time, Pallas kernels for 0%

commit v1 on v0

--- a/solution.py
+++ b/solution.py
@@ -9,11 +9,17 @@
 EPSILON = 1e-05
 
 
+def gather_and_add(x, axis):
+    parts = lax.all_gather(x, axis, axis=0, tiled=False)
+    acc = parts.sum(axis=0)
+    return acc
+
+
 def marker_moments(genotypes, samples):
     totals = jnp.sum(genotypes, axis=0, dtype=jnp.float32)
     center = lax.psum(totals, "smp") / samples
     local_squares = jnp.sum(jnp.square(genotypes.astype(jnp.float32) - center[None, :]), axis=0)
-    spread = lax.psum(local_squares, "smp") / samples
+    spread = gather_and_add(local_squares, "smp") / samples
     return lax.rsqrt(spread + EPSILON)
 
 

time: 167 us -> 170 us (1.018)
  blocking collectives: 42.3 us -> 46.9 us
    all_gather x0 -> x1, blocking collectives: none -> 13.1 us  [gather_and_add(): parts = lax.all_gather(x, axis, axis=0, tiled=False)]
    psum x1 -> x0, blocking collectives: 8.51 us -> none  [marker_moments(): spread = lax.psum(local_squares, 'smp') / samples]
where the time goes in v1:
time: 170 us
  waiting for transfers between devices  85.9 us (51%)
  blocking collectives  46.9 us (28%)
  between operations  13.2 us (8%)
  matrix products  12.8 us (8%)
  other arithmetic  11 us (6%)
    reduce_scatter x2, waiting for transfers between devices, shards(): lax.psum_scatter(lax.dot_general(standard, columns, (((0,), (0,)), ((), (...  51.3 us
    psum x1, waiting for transfers between devices, shards(): phenotype = lax.psum(partial_sum, 'mrk')  34.6 us
    psum x1, blocking collectives, marker_moments(): center = lax.psum(totals, 'smp') / samples  13.7 us
    all_gather x1, blocking collectives, gather_and_add(): parts = lax.all_gather(x, axis, axis=0, tiled=False)  13.1 us
    psum x1, blocking collectives, standardize(): center = lax.psum(totals, 'smp') / samples  11.7 us
    psum x1, blocking collectives, standardize(): spread = lax.psum(local_squares, 'smp') / samples  8.37 us
    dot_general x2, matrix products, shards(): lax.dot_general(standard, columns, (((0,), (0,)), ((), ())), preferred_el...  7.07 us
    dot_general x1, matrix products, shards(): partial_sum = jnp.dot(genotypes, scaled, preferred_element_type=jnp.float32)  5.77 us
  transfers between devices with their start and end apart: 3, of which 3 were waited for; matrix products, arithmetic and copies ran while one was open for 2% of the time, Pallas kernels for 0%

profile of v1, /device:TPU:0, one launch (start us, length us, event | category | flops | bytes accessed | tf_op | source)
XLA Modules:
  0.0 170.0 jit_solution(1480987931171910487)
XLA Ops:
  6.5 0.0 copy-start
  6.5 0.0 all-reduce.2.cloned.1.call-start
  6.5 2.9 %convert_reduce_fusion = f32[2048]{0:T(1024)S(1)} fusion(bf16[1024,2048]{1,0:T(8,128)(2,1)} %param.3), kind=kLoop, calls=%fused_computation.1 | loop fusion | flops 4192256 | bytes 4202496 | tf_op jit(solution)/shard_map/reduce_sum | solution.py:19
  9.4 13.7 %psum.28 = f32[2048]{0:T(1024)S(1)} all-reduce(f32[2048]{0:T(1024)S(1)} %convert_reduce_fusion), channel_id=1, replica_groups=mesh['grp'=2,'smp'=4,'mrk'=4] {'smp'}, use_global_device_ids=true, to_apply=%region_1.0 | all-reduce | flops 2048 | bytes 16384 | tf_op jit(solution)/shard_map/psum | solution.py:20
  23.2 3.3 %fusion.1 = f32[2048]{0:T(1024)S(1)} fusion(bf16[1024,2048]{1,0:T(8,128)(2,1)} %param.3, f32[2048]{0:T(1024)S(1)} %broadcast_multiply_fusion), kind=kLoop, calls=%fused_computation.3 | loop fusion | flops 8386560 | bytes 4210688 | tf_op jit(solution)/shard_map/reduce_sum | solution.py:21
  26.5 13.1 %all-gather = f32[8192]{0:T(1024)S(1)} all-gather(f32[2048]{0:T(1024)S(1)} %fusion.1), channel_id=2, replica_groups=mesh['grp'=2,'smp'=4,'mrk'=4] {'smp'}, dimensions={0}, use_global_device_ids=true | all-gather | bytes 40960 | tf_op jit(solution)/shard_map/all_gather | solution.py:13
  39.7 0.0 copy-done
  39.7 0.0 copy-done.2
  39.7 5.8 %convolution_bitcast_fusion = f32[1024,256]{0,1:T(8,128)} fusion(bf16[1024,2048]{1,0:T(8,128)(2,1)} %param.3, bf16[512,256]{1,0:T(8,128)(2,1)S(1)} %copy-done, s32[2048]{0:T(1024)S(1)} %copy-done.2, f32[2048]{0:T(1024)S(1)} %add_rsqrt_fusion), kind=kOutput, calls=%fused_computation.13 | convolution fusion | flops 1612709888 | bytes 5521408 | tf_op jit(solution)/shard_map/dot_general | solution.py:44
  45.5 0.0 all-reduce.2.cloned.1.call-update
  45.5 0.0 reduce-scatter.3.cloned.1.call-start
  45.6 34.6 %all-reduce.2.cloned.1.call-done = f32[1024,256]{0,1:T(8,128)} async-done(((f32[1024,256]{0,1:T(8,128)}), f32[1024,256]{0,1:T(8,128)}) %all-reduce.2.cloned.1.call-update) | async-done | bytes 1048592 | tf_op jit(solution)/shard_map/psum | solution.py:45
  80.2 1.4 reduce_sum.48
  81.6 11.7 %psum.30 = f32[256]{0:T(256)S(1)} all-reduce(f32[256]{0:T(256)S(1)} %reduce_sum.48), channel_id=1, replica_groups=mesh['grp'=2,'smp'=4,'mrk'=4] {'smp'}, use_global_device_ids=true, to_apply=%region_6.0 | all-reduce | flops 256 | bytes 2048 | tf_op jit(solution)/shard_map/psum | solution.py:28
  93.3 1.5 multiply_reduce_fusion
  94.8 8.4 %psum.31 = f32[256]{0:T(256)S(1)} all-reduce(f32[256]{0:T(256)S(1)} %multiply_reduce_fusion), channel_id=1, replica_groups=mesh['grp'=2,'smp'=4,'mrk'=4] {'smp'}, use_global_device_ids=true, to_apply=%region_8.0 | all-reduce | flops 256 | bytes 2048 | tf_op jit(solution)/shard_map/psum | solution.py:30
  103.2 3.7 %fusion.7 = f32[256,1024]{1,0:T(8,128)} fusion(bf16[1024,2048]{1,0:T(8,128)(2,1)} %param.3, f32[1024,256]{0,1:T(8,128)} %all-reduce.2.cloned.1.call-done, f32[256]{0:T(256)S(1)} %add_rsqrt_fusion.1, f32[256]{0:T(256)S(1)} %broadcast_multiply_fusion.1), kind=kOutput, calls=%fused_computation.10 | convolution fusion | flops 537657344 | bytes 4196352 | tf_op jit(solution)/shard_map/dot_general | solution.py:53
  106.9 0.0 reduce-scatter.3.cloned.1.call-update
  106.9 0.0 reduce-scatter.5.cloned.1.call-start
  106.9 3.4 %fusion.5 = f32[256,1024]{1,0:T(8,128)} fusion(bf16[1024,2048]{1,0:T(8,128)(2,1)} %param.3, f32[1024,256]{0,1:T(8,128)S(1)} %copy-done.1, f32[256]{0:T(256)S(1)} %add_rsqrt_fusion.1, f32[256]{0:T(256)S(1)} %broadcast_multiply_fusion.1), kind=kOutput, calls=%fused_computation.8 | convolution fusion | flops 537657344 | bytes 4196352 | tf_op jit(solution)/shard_map/dot_general | solution.py:53
  110.3 0.0 reduce-scatter.5.cloned.1.call-update
  110.4 23.1 %reduce-scatter.3.cloned.1.call-done = f32[64,1024]{1,0:T(8,128)} async-done(((f32[256,1024]{1,0:T(8,128)}), f32[64,1024]{1,0:T(8,128)}) %reduce-scatter.3.cloned.1.call-update) | async-done | bytes 262160 | tf_op jit(solution)/shard_map/reduce_scatter | solution.py:52
  133.5 28.1 %reduce-scatter.5.cloned.1.call-done = f32[64,1024]{1,0:T(8,128)} async-done(((f32[256,1024]{1,0:T(8,128)}), f32[64,1024]{1,0:T(8,128)}) %reduce-scatter.5.cloned.1.call-update) | async-done | bytes 262160 | tf_op jit(solution)/shard_map/reduce_scatter | solution.py:52
  161.6 1.9 %fusion.10 = f32[64,2048]{1,0:T(8,128)} fusion(f32[64,1024]{1,0:T(8,128)} %reduce-scatter.5.cloned.1.call-done, f32[64,1024]{1,0:T(8,128)} %reduce-scatter.3.cloned.1.call-done, f32[2048]{0:T(1024)S(1)} %add_rsqrt_fusion), kind=kLoop, calls=%fused_computation.17 | loop fusion | flops 393216 | bytes 1056768 | tf_op jit(solution)/shard_map/div | solution.py:62
  (9 shorter events, 0.1 us)
Async XLA Ops:
  6.5 33.2 %copy-start = (bf16[512,256]{1,0:T(8,128)(2,1)S(1)}, bf16[512,256]{1,0:T(8,128)(2,1)}, u32[]{:S(2)}) copy-start(bf16[512,256]{1,0:T(8,128)(2,1)} %param.5) | copy-start | bytes 786436
  6.5 33.2 %copy-start.2 = (s32[2048]{0:T(1024)S(1)}, s32[2048]{0:T(1024)}, u32[]{:S(2)}) copy-start(s32[2048]{0:T(1024)} %param.4) | copy-start | bytes 24580
  6.5 73.6 %all-reduce.2.cloned.1.call-start = ((), (), s32[]{:S(2)}) async-start(), calls=%async_computation.2 | async-start | bytes 2097152 | tf_op jit(solution)/shard_map/psum | solution.py:45
  45.5 88.0 %reduce-scatter.3.cloned.1.call-start = ((), (), s32[]{:S(2)}) async-start(), calls=%async_computation.3 | async-start | bytes 1310720 | tf_op jit(solution)/shard_map/reduce_scatter | solution.py:52
  80.2 26.8 %copy-start.1 = (f32[1024,256]{0,1:T(8,128)S(1)}, f32[1024,256]{0,1:T(8,128)}, u32[]{:S(2)}) copy-start(f32[1024,256]{0,1:T(8,128)} %all-reduce.2.cloned.1.call-done) | copy-start | bytes 3145732
  106.9 54.7 %reduce-scatter.5.cloned.1.call-start = ((), (), s32[]{:S(2)}) async-start(), calls=%async_computation.4 | async-start | bytes 1310720 | tf_op jit(solution)/shard_map/reduce_scatter | solution.py:52
Sparse Core Ops, SparseCore 0:
  45.6 34.5 all-reduce.1
  107.0 26.4 reduce-scatter.2
  135.8 25.7 reduce-scatter.4
